TPU v7x, 32 devices: a whole 2x2x4 slice. The times are simulated.
32 devices in a mesh: dp: 8 (over y, x, core), tensor: 4 (over z).
Axes of the slice: x: 2, y: 2, z: 4, core: 2. Of those that a mesh axis runs over, the one named last changes fastest.
Arguments:
- tokens: bfloat16 [32, 1024, 512], P(('dp', 'tensor')), may hold values from -6 to 6
- timestep: int32 [32], P(('dp', 'tensor')), may hold values from 0 to 999
- segment_ids: int32 [32, 1024], P('dp'), may hold values from 0 to 7, never falling along the last dimension, each value on 1 to 512 neighbouring positions
- span_lengths: int32 [32], P('dp'), may hold values from 512 to 1024
- w_qkv: float32 [3, 512, 512], P(None, 'dp', 'tensor'), may hold values from -0.25 to 0.25
- w_out_t: float32 [512, 512], P('dp', 'tensor'), may hold values from -1.5 to 1.5
- w_up: float32 [512, 2048], P('dp', 'tensor'), may hold values from -0.25 to 0.25
- w_down_t: float32 [512, 2048], P('dp', 'tensor'), may hold values from -0.125 to 0.125
- w_time: float32 [512, 512], replicated, may hold values from -0.25 to 0.25
- b_time: float32 [512], replicated, may hold values from -3 to 3
- ln1_gain: float32 [512], replicated, may hold values from 0.1 to 1.9
- ln1_bias: float32 [512], replicated, may hold values from -3 to 3
- ln2_gain: float32 [512], replicated, may hold values from 0.1 to 1.9
- ln2_bias: float32 [512], replicated, may hold values from -3 to 3
- b_up: float32 [2048], replicated, may hold values from -3 to 3
- b_down: float32 [512], replicated, may hold values from -3 to 3
- cotangent: bfloat16 [32, 1024, 512], P(('dp', 'tensor')), may hold values from -6 to 6
Outputs:
- layer_out: bfloat16 [32, 1024, 512], P(('dp', 'tensor'))
- grad_tokens: float32 [32, 1024, 512], P(('dp', 'tensor'))
- grad_w_qkv: float32 [3, 512, 512], P(None, 'dp', 'tensor')
- grad_w_out_t: float32 [512, 512], P('dp', 'tensor')
- grad_w_up: float32 [512, 2048], P('dp', 'tensor')
- grad_w_down_t: float32 [512, 2048], P('dp', 'tensor')
- grad_w_time: float32 [512, 512], replicated
- grad_b_time: float32 [512], replicated
- grad_ln1_gain: float32 [512], replicated
- grad_ln1_bias: float32 [512], replicated
- grad_ln2_gain: float32 [512], replicated
- grad_ln2_bias: float32 [512], replicated
- grad_b_up: float32 [2048], replicated
- grad_b_down: float32 [512], replicated
Inputs may be any that keep to these rules, and one draw needn't show every extreme that they name: `segment_ids`: never falls along a row; each document has 1 to 512 positions and one has exactly that many.
All inputs are finite; a program needn't handle non-finite values.
Results may differ from a plain program's by a relative error of at most 0.013.
Values may be sent and summed in bfloat16 or wider, within the bound.
A program may use at most 192 MiB of HBM per device.

v0:
```python
import math
import jax
import jax.numpy as jnp
from jax import lax
from jax.sharding import PartitionSpec as P

HS = 64
FF = 2048
highest = lax.Precision.HIGHEST
epsilon = 1e-05
masked_score = -1e30


def split_up(value, dim, count):
    before, after = (value.shape[:dim], value.shape[dim + 1 :])
    return jnp.moveaxis(value.reshape(*before, count, -1, *after), dim, 0)


def sent_and_summed(value, axis, dim):
    count = lax.axis_size(axis)
    parts = lax.all_to_all(split_up(value, dim, count), axis, 0, 0, tiled=True)
    return jnp.sum(parts.astype(jnp.float32), axis=0)


def side_by_side(arrays, axis, dim, along):
    ends, at = ([], 0)
    for a in arrays[:-1]:
        at += a.shape[along]
        ends.append(at)
    both = jnp.concatenate(arrays, axis=along)
    return tuple(jnp.split(sent_and_summed(both, axis, dim), ends, axis=along))


def norm_layer(values, gain_vec, shift_vec):
    row_mean = jnp.mean(values, axis=-1, keepdims=True)
    centred = values - row_mean
    variance = jnp.mean(centred * centred, axis=-1, keepdims=True)
    return centred * lax.rsqrt(variance + epsilon) * gain_vec + shift_vec


def time_features(timestep, features):
    half_width = features // 2
    frequency = jnp.exp(-math.log(10000.0) * jnp.arange(half_width, dtype=jnp.float32) / half_width)
    angles = timestep.astype(jnp.float32)[:, None] * frequency[None, :]
    return jnp.concatenate([jnp.sin(angles), jnp.cos(angles)], axis=1)


def allowed_keys(segment, length):
    places = jnp.arange(segment.shape[0], dtype=jnp.int32)
    same_doc = segment[:, None] == segment[None, :]
    is_valid = (places < length)[None, :] | (places[:, None] == places[None, :])
    return same_doc & is_valid


def gelu_tanh(values):
    return jax.nn.gelu(values, approximate=True)


def split_heads(values):
    return values.reshape(values.shape[0], values.shape[1] // HS, HS)


def head_scores(query_heads, key_heads, allowed):
    scores = jnp.einsum(
        "qhe,khe->hqk", query_heads, key_heads, preferred_element_type=jnp.float32
    ) * (1.0 / math.sqrt(HS))
    return jnp.where(allowed[None], scores, masked_score)


def attend_forward(packed):
    query_heads = split_heads(packed[0])
    key_heads = split_heads(packed[1])
    value_heads = split_heads(packed[2])
    scores = head_scores(query_heads, key_heads, allowed_keys(packed[3], packed[4]))
    row_max = jnp.max(scores, axis=-1, keepdims=True)
    raised = jnp.exp(scores - row_max)
    row_total = jnp.sum(raised, axis=-1, keepdims=True)
    probs_low = (raised / row_total).astype(jnp.bfloat16)
    mixed = jnp.einsum("hqk,khe->qhe", probs_low, value_heads, preferred_element_type=jnp.float32)
    return (mixed.reshape(packed[0].shape).astype(jnp.bfloat16), row_max + jnp.log(row_total))


def attend_backward(packed):
    query_heads = split_heads(packed[0])
    key_heads = split_heads(packed[1])
    value_heads = split_heads(packed[2])
    grad_heads = split_heads(packed[3])
    scores = head_scores(query_heads, key_heads, allowed_keys(packed[5], packed[6]))
    attn_probs = jnp.exp(scores - packed[4])
    probs_low = attn_probs.astype(jnp.bfloat16)
    grad_values = jnp.einsum(
        "hqk,qhe->khe", probs_low, grad_heads, preferred_element_type=jnp.float32
    )
    grad_probs = jnp.einsum(
        "qhe,khe->hqk", grad_heads, value_heads, preferred_element_type=jnp.float32
    )
    row_delta = jnp.sum(attn_probs * grad_probs, axis=-1, keepdims=True)
    grad_scores = (attn_probs * (grad_probs - row_delta)).astype(jnp.bfloat16)
    score_scale = 1.0 / math.sqrt(HS)
    grad_queries = (
        jnp.einsum("hqk,khe->qhe", grad_scores, key_heads, preferred_element_type=jnp.float32)
        * score_scale
    )
    grad_keys = (
        jnp.einsum("hqk,qhe->khe", grad_scores, query_heads, preferred_element_type=jnp.float32)
        * score_scale
    )
    shape_rows = packed[0].shape
    return jnp.stack(
        [
            grad_queries.reshape(shape_rows),
            grad_keys.reshape(shape_rows),
            grad_values.reshape(shape_rows),
        ]
    ).astype(jnp.bfloat16)


def shards(
    tokens,
    timestep,
    segment_ids,
    span_lengths,
    w_qkv,
    w_out_t,
    w_up,
    w_down_t,
    w_time,
    b_time,
    ln1_gain,
    ln1_bias,
    ln2_gain,
    ln2_bias,
    b_up,
    b_down,
    cotangent,
):

    def whole(w, dim):
        w = lax.all_gather(w.astype(jnp.bfloat16), "tensor", axis=dim + 1, tiled=True)
        return lax.all_gather(w, "dp", axis=dim, tiled=True)

    def part(g, dim):
        g = lax.psum_scatter(g.astype(jnp.bfloat16), "dp", scatter_dimension=dim, tiled=True)
        return lax.psum_scatter(g, "tensor", scatter_dimension=dim + 1, tiled=True).astype(
            jnp.float32
        )

    qkv_copy, out_copy, up_copy, down_copy = (
        whole(w_qkv, 1),
        whole(w_out_t, 0),
        whole(w_up, 0),
        whole(w_down_t, 0),
    )
    row = lax.axis_index("tensor")
    rows = tokens.shape[0]
    own_ids = lax.dynamic_slice_in_dim(segment_ids, row * rows, rows, 0)
    own_len = lax.dynamic_slice_in_dim(span_lengths, row * rows, rows, 0)
    time_emb = time_features(timestep, tokens.shape[2])
    time_proj = jnp.dot(time_emb, w_time, precision=highest) + b_time
    start = tokens.astype(jnp.float32) + time_proj[:, None, :]
    normed_one = norm_layer(start, ln1_gain, ln1_bias).astype(jnp.bfloat16)
    qkv_act = jnp.einsum(
        "nsd,cde->cnse", normed_one, qkv_copy, preferred_element_type=jnp.float32
    ).astype(jnp.bfloat16)
    mixed, log_total = lax.map(
        attend_forward, (qkv_act[0], qkv_act[1], qkv_act[2], own_ids, own_len)
    )
    attn_out = jnp.einsum("nse,de->nsd", mixed, out_copy, preferred_element_type=jnp.float32)
    middle = start + attn_out
    normed_two = norm_layer(middle, ln2_gain, ln2_bias).astype(jnp.bfloat16)
    upper = (
        jnp.einsum("nsd,df->nsf", normed_two, up_copy, preferred_element_type=jnp.float32) + b_up
    )
    activated = gelu_tanh(upper).astype(jnp.bfloat16)
    ffn_out = jnp.einsum("nsf,df->nsd", activated, down_copy, preferred_element_type=jnp.float32)
    layer_out = (middle + ffn_out + b_down).astype(jnp.bfloat16)
    grad_b_down = jnp.sum(cotangent.astype(jnp.float32), axis=(0, 1))
    grad_down = jnp.einsum("nsd,nsf->df", cotangent, activated, preferred_element_type=jnp.float32)
    grad_act = jnp.einsum("nsd,df->nsf", cotangent, down_copy, preferred_element_type=jnp.float32)
    gelu_value, gelu_pull = jax.vjp(gelu_tanh, upper)
    grad_upper = gelu_pull(grad_act)[0].astype(jnp.bfloat16)
    grad_bias_up = jnp.sum(grad_upper.astype(jnp.float32), axis=(0, 1))
    grad_up = jnp.einsum("nsd,nsf->df", normed_two, grad_upper, preferred_element_type=jnp.float32)
    grad_normed_two = jnp.einsum(
        "nsf,df->nsd", grad_upper, up_copy, preferred_element_type=jnp.float32
    )
    norm_two_value, norm_two_pull = jax.vjp(norm_layer, middle, ln2_gain, ln2_bias)
    grad_middle_norm, grad_gain_two, grad_bias_two = norm_two_pull(grad_normed_two)
    grad_middle = cotangent.astype(jnp.float32) + grad_middle_norm
    grad_attn = grad_middle.astype(jnp.bfloat16)
    grad_out_w = jnp.einsum("nsd,nse->de", grad_attn, mixed, preferred_element_type=jnp.float32)
    grad_mixed = jnp.einsum(
        "nsd,de->nse", grad_attn, out_copy, preferred_element_type=jnp.float32
    ).astype(jnp.bfloat16)
    grad_qkv_act = lax.map(
        attend_backward,
        (qkv_act[0], qkv_act[1], qkv_act[2], grad_mixed, log_total, own_ids, own_len),
    )
    grad_qkv_w = jnp.einsum(
        "nsd,ncse->cde", normed_one, grad_qkv_act, preferred_element_type=jnp.float32
    )
    grad_normed_one = jnp.einsum(
        "ncse,cde->nsd", grad_qkv_act, qkv_copy, preferred_element_type=jnp.float32
    )
    norm_one_value, norm_one_pull = jax.vjp(norm_layer, start, ln1_gain, ln1_bias)
    grad_start_norm, grad_gain_one, grad_bias_one = norm_one_pull(grad_normed_one)
    grad_tokens = grad_middle + grad_start_norm
    grad_time_rows = jnp.sum(grad_tokens, axis=1)
    lines = jnp.concatenate([time_emb, grad_time_rows], axis=1)
    lines = lax.all_gather(lines, ("dp", "tensor"), axis=0, tiled=True)
    all_emb, all_grad = (lines[:, : time_emb.shape[1]], lines[:, time_emb.shape[1] :])
    grad_time_w = jnp.dot(all_emb.T, all_grad, precision=highest)
    grad_time_bias = jnp.sum(all_grad, axis=0)
    small = jnp.concatenate(
        [grad_gain_one, grad_bias_one, grad_gain_two, grad_bias_two, grad_b_down, grad_bias_up]
    )
    small = lax.psum(small, ("dp", "tensor"))
    cuts = jnp.split(small, [tokens.shape[2] * k for k in range(1, 6)])
    return (
        layer_out,
        grad_tokens,
        part(grad_qkv_w, 1),
        part(grad_out_w, 0),
        part(grad_up, 0),
        part(grad_down, 0),
        grad_time_w,
        grad_time_bias,
        cuts[0],
        cuts[1],
        cuts[2],
        cuts[3],
        cuts[5],
        cuts[4],
    )


def solution(mesh):
    return jax.shard_map(
        shards,
        mesh=mesh,
        in_specs=(
            P(("dp", "tensor"), None, None),
            P(("dp", "tensor")),
            P("dp", None),
            P("dp"),
            P(None, "dp", "tensor"),
            P("dp", "tensor"),
            P("dp", "tensor"),
            P("dp", "tensor"),
            P(),
            P(),
            P(),
            P(),
            P(),
            P(),
            P(),
            P(),
            P(("dp", "tensor"), None, None),
        ),
        out_specs=(
            P(("dp", "tensor"), None, None),
            P(("dp", "tensor"), None, None),
            P(None, "dp", "tensor"),
            P("dp", "tensor"),
            P("dp", "tensor"),
            P("dp", "tensor"),
            P(),
            P(),
            P(),
            P(),
            P(),
            P(),
            P(),
            P(),
        ),
        check_vma=False,
    )
```

profile of v0, /device:TPU:0, one launch (start us, length us, event | category | flops | bytes accessed | tf_op | source)
XLA Modules:
  0.0 517.9 jit_solution(3765666602704823875)
XLA Ops:
  7.3 1.0 convert_element_type.127
  8.3 14.8 %all_gather.27 = bf16[3,64,512]{2,1,0:T(8,128)(2,1)} all-gather(bf16[3,64,128]{2,1,0:T(8,128)(2,1)S(1)} %convert_element_type.127), channel_id=1, replica_groups=mesh['dp'=8,'tensor'=4] {'tensor'}, dimensions={2}, use_global_device_ids=true | all-gather | bytes 245760 | tf_op jit(solution)/shard_map/all_gather | solution.py:139
  23.2 0.9 convert_element_type.138
  24.1 15.1 %all_gather.31 = bf16[64,2048]{1,0:T(8,128)(2,1)} all-gather(bf16[64,512]{1,0:T(8,128)(2,1)S(1)} %convert_element_type.138), channel_id=1, replica_groups=mesh['dp'=8,'tensor'=4] {'tensor'}, dimensions={1}, use_global_device_ids=true | all-gather | bytes 327680 | tf_op jit(solution)/shard_map/all_gather | solution.py:139
  39.3 0.9 convert_element_type.140
  40.2 14.9 %all_gather.33 = bf16[64,2048]{1,0:T(8,128)(2,1)} all-gather(bf16[64,512]{1,0:T(8,128)(2,1)S(1)} %convert_element_type.140), channel_id=1, replica_groups=mesh['dp'=8,'tensor'=4] {'tensor'}, dimensions={1}, use_global_device_ids=true | all-gather | bytes 327680 | tf_op jit(solution)/shard_map/all_gather | solution.py:139
  57.2 0.7 constant_dynamic-slice_fusion.1
  58.0 12.0 %all_gather.29 = bf16[64,512]{1,0:T(8,128)(2,1)S(1)} all-gather(bf16[64,128]{1,0:T(8,128)(2,1)S(1)} %convert_element_type.136), channel_id=1, replica_groups=mesh['dp'=8,'tensor'=4] {'tensor'}, dimensions={1}, use_global_device_ids=true | all-gather | bytes 81920 | tf_op jit(solution)/shard_map/all_gather | solution.py:139
  69.9 11.6 %all_gather.30 = bf16[512,512]{1,0:T(8,128)(2,1)} all-gather(bf16[64,512]{1,0:T(8,128)(2,1)S(1)} %all_gather.29), channel_id=1, replica_groups=mesh['dp'=8,'tensor'=4] {'dp'}, dimensions={0}, use_global_device_ids=true | all-gather | bytes 589824 | tf_op jit(solution)/shard_map/all_gather | solution.py:140
  84.5 2.3 fusion.14
  86.8 3.5 convert_bitcast_fusion
  90.7 1.0 copy-done.15
  91.7 14.0 %fusion.59 = (f32[8,1024]{1,0:T(8,128)S(1)}, f32[8,1024,1024]{1,2,0:T(8,128)}) fusion(bf16[1024,8,64]{0,2,1:T(8,128)(2,1)S(1)} %bitcast.135, bf16[1024,8,64]{0,2,1:T(8,128)(2,1)S(1)} %bitcast.133, pred[1024,1024]{0,1:T(8,128)(4,1)S(1)} %copy-done.15), kind=kOutput, calls=%fused_computation.112 | convolution fusion | flops 1098899456 | bytes 36732928 | tf_op jit(solution)/shard_map/while/body/eval_jaxpr/qhe,khe->hqk/dot_general | solution.py:64
  105.7 13.1 %fusion = f32[8,1024]{1,0:T(8,128)S(1)} fusion(f32[8,1024,1024]{1,2,0:T(8,128)} %get-tuple-element.125, f32[8,1024]{1,0:T(8,128)S(1)} %get-tuple-element.124), kind=kLoop, calls=%fused_computation.6 | loop fusion | flops 16769024 | bytes 33619968 | tf_op jit(solution)/shard_map/while/body/eval_jaxpr/reduce_sum | solution.py:77
  118.8 14.0 %fusion.29 = bf16[8,64,1024]{2,1,0:T(8,128)(2,1)S(1)} fusion(bf16[1024,8,64]{0,2,1:T(8,128)(2,1)S(1)} %bitcast.140, f32[8,1024,1024]{1,2,0:T(8,128)} %get-tuple-element.125, f32[8,1024]{1,0:T(8,128)S(1)} %fusion, f32[8,1024]{1,0:T(8,128)S(1)} %get-tuple-element.124), kind=kOutput, calls=%fused_computation.62 | convolution fusion | flops 1099431936 | bytes 35717120 | tf_op jit(solution)/shard_map/while/body/eval_jaxpr/hqk,khe->qhe/dot_general | solution.py:79
  132.9 0.8 fusion.60
  133.9 1.3 copy-done.5
  135.6 11.5 %multiply_convert_fusion.1 = (bf16[1024,2048]{1,0:T(8,128)(2,1)}, f32[1024,2048]{1,0:T(8,128)}) fusion(f32[2048]{0:T(1024)S(1)} %copy-done.46, bf16[512,2048]{1,0:T(8,128)(2,1)} %all-gather.7.cloned.1.call-done, f32[1,1024,512]{1,2,0:T(8,128)} %copy-done.5, f32[512]{0:T(512)S(1)} %copy-done.49, f32[512]{0:T(512)S(1)} %copy-done.43, f32[1024]{0:T(1024)S(1)} %fusion.40, ...), kind=kOutput, calls=%fused_computation.21 | convolution fusion | flops 2171076608 | bytes 16797696 | tf_op jit(solution)/shard_map/nsd,df->nsf/dot_general | solution.py:172
  147.1 10.2 %convert_reduce_fusion = (f32[2048]{0:T(1024)S(1)}, bf16[1024,2048]{1,0:T(8,128)(2,1)S(1)}) fusion(f32[1024,2048]{1,0:T(8,128)} %get-tuple-element.129, f32[2048]{0:T(1024)S(1)} %copy-done.46, bf16[512,2048]{1,0:T(8,128)(2,1)} %all-gather.9.cloned.1.call-done, bf16[1,1024,512]{2,1,0:T(8,128)(2,1)S(1)} %copy-done.24), kind=kOutput, calls=%fused_computation.20 | convolution fusion | flops 2195716096 | bytes 15745024 | tf_op jit(solution)/shard_map/nsd,df->nsf/dot_general | solution.py:179
  157.3 3.7 fusion.62
  161.0 3.0 copy.79
  164.0 3.0 fusion.16
  168.5 0.9 copy-done.3
  169.4 0.7 copy-done.53
  170.0 1.6 convolution_convert_fusion.4
  171.6 2.0 convolution_convert_fusion.3
  173.6 14.4 %fusion.25 = bf16[8,64,1024]{2,1,0:T(8,128)(2,1)} fusion(bf16[1024,8,64]{0,2,1:T(8,128)(2,1)S(1)} %bitcast.138, f32[8,1024,1024]{1,2,0:T(8,128)} %get-tuple-element.125, f32[8,1024]{1,0:T(8,128)S(1)} %log_add_fusion), kind=kOutput, calls=%fused_computation.59 | convolution fusion | flops 1091043328 | bytes 35684352 | tf_op jit(solution)/shard_map/while/body/eval_jaxpr/hqk,qhe->khe/dot_general | solution.py:91
  188.0 22.0 %multiply_reduce_fusion = (f32[8,1024]{1,0:T(8,128)S(1)}, f32[8,1024,1024]{1,2,0:T(8,128)}) fusion(f32[8,1024,1024]{1,2,0:T(8,128)} %get-tuple-element.125, f32[8,1024]{1,0:T(8,128)S(1)} %log_add_fusion, bf16[1024,8,64]{0,2,1:T(8,128)(2,1)S(1)} %bitcast.139, bf16[1024,8,64]{0,2,1:T(8,128)(2,1)S(1)} %bitcast.141), kind=kOutput, calls=%fused_computation.1 | convolution fusion | flops 1098899456 | bytes 69271552 | tf_op jit(solution)/shard_map/while/body/eval_jaxpr/qhe,khe->hqk/dot_general | solution.py:94
  210.1 28.7 %multiply_convert_fusion = bf16[8,1024,1024]{1,2,0:T(8,128)(2,1)} fusion(f32[8,1024,1024]{1,2,0:T(8,128)} %get-tuple-element.131, f32[8,1024,1024]{1,2,0:T(8,128)} %get-tuple-element.125, f32[8,1024]{1,0:T(8,128)S(1)} %get-tuple-element.130, f32[8,1024]{1,0:T(8,128)S(1)} %log_add_fusion), kind=kLoop, calls=%fused_computation | loop fusion | flops 33554432 | bytes 83951616 | tf_op jit(solution)/shard_map/while/body/eval_jaxpr/convert_element_type | solution.py:98
  238.9 12.1 %multiply_convert_fusion.2 = bf16[8,64,1024]{2,1,0:T(8,128)(2,1)} fusion(bf16[1024,8,64]{0,2,1:T(8,128)(2,1)S(1)} %bitcast.136, bf16[8,1024,1024]{1,2,0:T(8,128)(2,1)} %multiply_convert_fusion), kind=kOutput, calls=%fused_computation.47 | convolution fusion | flops 1074790400 | bytes 18874368 | tf_op jit(solution)/shard_map/while/body/eval_jaxpr/hqk,qhe->khe/dot_general | solution.py:105
  250.9 9.9 %multiply_convert_fusion.3 = bf16[8,64,1024]{2,1,0:T(8,128)(2,1)} fusion(bf16[1024,8,64]{0,2,1:T(8,128)(2,1)S(1)} %bitcast.134, bf16[8,1024,1024]{1,2,0:T(8,128)(2,1)} %multiply_convert_fusion), kind=kOutput, calls=%fused_computation.48 | convolution fusion | flops 1074790400 | bytes 18874368 | tf_op jit(solution)/shard_map/while/body/eval_jaxpr/hqk,khe->qhe/dot_general | solution.py:101
  260.8 1.3 copy.85
  262.1 2.4 copy.83
  264.5 1.3 copy.84
  265.9 4.8 fusion.28
  270.7 4.4 copy.89
  275.2 6.7 %convolution_convert_fusion.1 = bf16[512,2048]{1,0:T(8,128)(2,1)} fusion(bf16[1024,2048]{1,0:T(8,128)(2,1)} %copy-done.55, f32[1,1024,512]{1,2,0:T(8,128)} %copy-done.5, f32[512]{0:T(512)S(1)} %copy-done.49, f32[512]{0:T(512)S(1)} %copy-done.43, f32[1024]{0:T(1024)S(1)} %fusion.40, f32[1024]{0:T(1024)S(1)} %broadcast_multiply_fusion), kind=kOutput, calls=%fused_computation.30 | convolution fusion | flops 2151153664 | bytes 8400896 | tf_op jit(solution)/shard_map/nsd,nsf->df/dot_general | solution.py:183
  282.1 0.9 copy-done.25
  283.1 6.0 %fusion.15 = bf16[512,2048]{0,1:T(8,128)(2,1)} fusion(bf16[1024,2048]{1,0:T(8,128)(2,1)} %get-tuple-element.128, bf16[1,1024,512]{2,1,0:T(8,128)(2,1)S(1)} %copy-done.25), kind=kOutput, calls=%fused_computation.31 | convolution fusion | flops 2148532224 | bytes 7340032 | tf_op jit(solution)/shard_map/nsd,nsf->df/dot_general | solution.py:178
  289.1 4.0 copy.110
  295.0 4.9 fusion.61
  299.9 2.9 copy.86
  302.8 2.3 fusion.18
  305.1 1.0 fusion.17
  306.9 2.6 fusion.55
  309.6 1.6 copy.108
  311.3 24.4 %all-reduce.3.cloned.1.call-done = bf16[3,512,512]{2,0,1:T(4,128)(2,1)} async-done(((bf16[3,512,512]{2,0,1:T(4,128)(2,1)}), bf16[3,512,512]{2,0,1:T(4,128)(2,1)}) %all-reduce.3.cloned.1.call-update) | async-done | bytes 1572880
  335.7 1.0 constant_dynamic-slice_fusion
  336.7 14.0 %copy.106 = bf16[3,64,512]{0,1,2:T(8,128)(2,1)} copy(bf16[3,64,512]{2,0,1:T(4,128)(2,1)S(1)} %constant_dynamic-slice_fusion) | data formatting | bytes 393216
  350.7 13.9 %reshape.435 = bf16[512,192]{1,0:T(8,128)(2,1)} reshape(bf16[512,64,3]{2,1,0:T(8,128)(2,1)} %bitcast.132) | data formatting | bytes 393216
  364.6 67.5 %all-gather = f32[32,1,1024]{2,1,0:T(1,128)S(1)} all-gather(f32[1,1,1024]{2,1,0:T(1,128)S(1)} %maximum_bitcast_fusion), channel_id=1, replica_groups=mesh['dp'=8,'tensor'=4] {'dp','tensor'}, dimensions={0}, use_global_device_ids=true | all-gather | bytes 135168 | tf_op jit(solution)/shard_map/all_gather | solution.py:210
  433.2 5.2 %fusion.21 = bf16[1,1024,512]{1,2,0:T(8,128)(2,1)S(1)} fusion(f32[1,1024,512]{1,2,0:T(8,128)S(1)} %copy-done.7, bf16[1024,2048]{1,0:T(8,128)(2,1)} %get-tuple-element.128, bf16[512,2048]{1,0:T(8,128)(2,1)} %all-gather.9.cloned.1.call-done, f32[512]{0:T(512)S(1)} %copy-done.50), kind=kOutput, calls=%fused_computation.44 | convolution fusion | flops 2149056512 | bytes 9439232 | tf_op jit(solution)/shard_map/nsf,df->nsd/dot_general | solution.py:175
  438.5 2.1 copy.111
  440.6 1.3 copy.92
  441.9 37.5 %psum.7 = f32[4608]{0:T(1024)S(1)} all-reduce(f32[4608]{0:T(1024)S(1)} %constant_dynamic-update-slice_fusion), channel_id=1, replica_groups=mesh['dp'=8,'tensor'=4] {'dp','tensor'}, use_global_device_ids=true, to_apply=%region_27.28 | all-reduce | flops 4608 | bytes 36864 | tf_op jit(solution)/shard_map/psum | solution.py:217
  480.0 1.8 copy.93
  482.4 2.0 fusion.36
  484.4 0.8 copy.109
  485.9 5.3 %reshape.436 = bf16[128,64,3]{2,1,0:T(8,128)(2,1)S(1)} reshape(bf16[128,192]{1,0:T(8,128)(2,1)} %reduce-scatter.22.cloned.1.call-done) | data formatting | bytes 98304
  491.2 2.2 copy.107
  493.4 0.7 copy.94
  494.1 1.5 convert_element_type.154
  495.6 13.7 %reduce-scatter.20.cloned.1.call-done = bf16[64,512]{0,1:T(8,128)(2,1)} async-done(((bf16[64,2048]{0,1:T(8,128)(2,1)}), bf16[64,512]{0,1:T(8,128)(2,1)}) %reduce-scatter.20.cloned.1.call-update) | async-done | bytes 65552 | tf_op jit(solution)/shard_map/reduce_scatter | solution.py:144
  509.3 1.6 copy.95
  (175 shorter events, 12.1 us)
Async XLA Ops:
  7.2 74.9 %copy-start = (f32[512,512]{1,0:T(8,128)S(1)}, f32[512,512]{1,0:T(8,128)}, u32[]{:S(2)}) copy-start(f32[512,512]{1,0:T(8,128)} %param.25) | copy-start | bytes 3145732
  7.2 48.7 %copy-start.51 = (s32[4]{0:T(128)S(1)}, s32[4]{0:T(128)}, u32[]{:S(2)}) copy-start(s32[4]{0:T(128)} %param.20) | copy-start | bytes 52
  7.2 50.7 %copy-start.36 = (f32[64,128]{1,0:T(8,128)S(1)}, f32[64,128]{1,0:T(8,128)}, u32[]{:S(2)}) copy-start(f32[64,128]{1,0:T(8,128)} %param.22) | copy-start | bytes 98308
  7.2 74.4 %copy-start.22 = (bf16[1,1024,512]{2,1,0:T(8,128)(2,1)S(1)}, bf16[1,1024,512]{2,1,0:T(8,128)(2,1)}, u32[]{:S(2)}) copy-start(bf16[1,1024,512]{2,1,0:T(8,128)(2,1)} %param.17) | copy-start | bytes 3145732
  7.2 79.6 %all-gather.5.cloned.1.call-start = ((), (), s32[]{:S(2)}) async-start(), calls=%async_computation.7 | async-start | bytes 1769472 | tf_op jit(solution)/shard_map/all_gather | solution.py:140
  23.1 112.4 %all-gather.7.cloned.1.call-start = ((), (), s32[]{:S(2)}) async-start(), calls=%async_computation.8 | async-start | bytes 2359296 | tf_op jit(solution)/shard_map/all_gather | solution.py:140
  39.2 107.9 %all-gather.9.cloned.1.call-start = ((), (), s32[]{:S(2)}) async-start(), calls=%async_computation.9 | async-start | bytes 2359296 | tf_op jit(solution)/shard_map/all_gather | solution.py:140
  55.1 27.6 %copy-start.44 = (f32[512]{0:T(512)S(1)}, f32[512]{0:T(512)}, u32[]{:S(2)}) copy-start(f32[512]{0:T(512)} %param.26) | copy-start | bytes 6148
  55.2 254.4 %reduce-scatter.14.cloned.1.call-start = ((), (), s32[]{:S(2)}) async-start(), calls=%async_computation.10 | async-start | bytes 589824 | tf_op jit(solution)/shard_map/reduce_scatter | solution.py:143
  57.2 25.6 %copy-start.41 = (f32[1,256]{1,0:T(1,128)}, f32[1,256]{1,0:T(1,128)S(1)}, u32[]{:S(2)}) copy-start(f32[1,256]{1,0:T(1,128)S(1)} %get-tuple-element.139) | copy-start | bytes 3076
  57.2 25.6 %copy-start.39 = (f32[1,256]{1,0:T(1,128)}, f32[1,256]{1,0:T(1,128)S(1)}, u32[]{:S(2)}) copy-start(f32[1,256]{1,0:T(1,128)S(1)} %get-tuple-element.138) | copy-start | bytes 3076
  82.7 1.2 copy-start.23
  83.1 3.7 copy-start.30
  83.1 3.7 copy-start.37
  83.1 3.7 copy-start.47
  83.5 6.8 %copy-start.34 = (f32[1024]{0:T(1024)}, f32[1024]{0:T(1024)S(1)}, u32[]{:S(2)}) copy-start(f32[1024]{0:T(1024)S(1)} %multiply_reduce_fusion.2) | copy-start | bytes 12292
  84.0 6.3 %copy-start.32 = (f32[1024]{0:T(1024)}, f32[1024]{0:T(1024)S(1)}, u32[]{:S(2)}) copy-start(f32[1024]{0:T(1024)S(1)} %fusion.39) | copy-start | bytes 12292
  84.5 83.5 %copy-start.13 = (bf16[1,1024,512]{1,2,0:T(8,128)(2,1)}, bf16[1,1024,512]{1,2,0:T(8,128)(2,1)S(1)}, u32[]{:S(2)}) copy-start(bf16[1,1024,512]{1,2,0:T(8,128)(2,1)S(1)} %copy.78) | copy-start | bytes 3145732
  90.3 1.4 copy-start.15
  90.6 15.0 %copy-start.9 = (bf16[1,1,1024,512]{2,3,0,1:T(8,128)(2,1)}, bf16[1,1,1024,512]{2,3,0,1:T(8,128)(2,1)S(1)}, u32[]{:S(2)}) copy-start(bf16[1,1,1024,512]{2,3,0,1:T(8,128)(2,1)S(1)} %get-tuple-element.115) | copy-start | bytes 3145732
  90.7 15.0 %copy-start.11 = (bf16[1,1,1024,512]{2,3,0,1:T(8,128)(2,1)}, bf16[1,1,1024,512]{2,3,0,1:T(8,128)(2,1)S(1)}, u32[]{:S(2)}) copy-start(bf16[1,1,1024,512]{2,3,0,1:T(8,128)(2,1)S(1)} %get-tuple-element.116) | copy-start | bytes 3145732
  90.7 28.1 %copy-start.17 = (bf16[1,1,1024,512]{2,3,0,1:T(8,128)(2,1)}, bf16[1,1,1024,512]{2,3,0,1:T(8,128)(2,1)S(1)}, u32[]{:S(2)}) copy-start(bf16[1,1,1024,512]{2,3,0,1:T(8,128)(2,1)S(1)} %get-tuple-element.117) | copy-start | bytes 3145732
  118.8 14.1 %copy-start.28 = (bf16[512,512]{1,0:T(8,128)(2,1)S(1)}, bf16[512,512]{1,0:T(8,128)(2,1)}, u32[]{:S(2)}) copy-start(bf16[512,512]{1,0:T(8,128)(2,1)} %all_gather.30) | copy-start | bytes 1572868
  133.8 1.3 copy-start.5
  133.8 1.7 copy-start.43
  133.8 1.7 copy-start.46
  133.8 1.7 copy-start.49
  135.5 11.6 %copy-start.24 = (bf16[1,1024,512]{2,1,0:T(8,128)(2,1)S(1)}, bf16[1,1024,512]{2,1,0:T(8,128)(2,1)}, u32[]{:S(2)}) copy-start(bf16[1,1024,512]{2,1,0:T(8,128)(2,1)} %param.33) | copy-start | bytes 3145732
  147.1 10.3 %copy-start.45 = (bf16[512,2048]{1,0:T(8,128)(2,1)S(1)}, bf16[512,2048]{1,0:T(8,128)(2,1)}, u32[]{:S(2)}) copy-start(bf16[512,2048]{1,0:T(8,128)(2,1)} %all-gather.7.cloned.1.call-done) | copy-start | bytes 6291460
  157.3 3.7 copy-start.55
  164.0 3.0 copy-start.6
  164.0 3.5 copy-start.8
  168.0 1.4 copy-start.3
  168.1 2.0 copy-start.53
  170.0 1.6 copy-start.21
  170.0 1.6 copy-start.29
  173.6 14.4 %copy-start.18 = (bf16[1,1,1024,512]{2,3,0,1:T(8,128)(2,1)S(1)}, bf16[1,1,1024,512]{2,3,0,1:T(8,128)(2,1)}, u32[]{:S(2)}) copy-start(bf16[1,1,1024,512]{2,3,0,1:T(8,128)(2,1)} %copy-done.17) | copy-start | bytes 3145732
  210.1 125.6 %all-reduce.3.cloned.1.call-start = ((), (), s32[]{:S(2)}) async-start(), calls=%async_computation.17 | async-start | bytes 4194304
  210.1 28.7 %copy-start.12 = (bf16[1,1,1024,512]{2,3,0,1:T(8,128)(2,1)S(1)}, bf16[1,1,1024,512]{2,3,0,1:T(8,128)(2,1)}, u32[]{:S(2)}) copy-start(bf16[1,1,1024,512]{2,3,0,1:T(8,128)(2,1)} %copy-done.11) | copy-start | bytes 3145732
  238.9 12.1 %copy-start.10 = (bf16[1,1,1024,512]{2,3,0,1:T(8,128)(2,1)S(1)}, bf16[1,1,1024,512]{2,3,0,1:T(8,128)(2,1)}, u32[]{:S(2)}) copy-start(bf16[1,1,1024,512]{2,3,0,1:T(8,128)(2,1)} %copy-done.9) | copy-start | bytes 3145732
  250.9 9.9 %copy-start.19 = (bf16[8,64,1024]{2,1,0:T(8,128)(2,1)S(1)}, bf16[8,64,1024]{2,1,0:T(8,128)(2,1)}, u32[]{:S(2)}) copy-start(bf16[8,64,1024]{2,1,0:T(8,128)(2,1)} %fusion.25) | copy-start | bytes 3145732
  260.8 3.7 copy-start.20
  262.1 3.7 copy-start.26
  262.1 3.7 copy-start.31
  262.1 3.7 copy-start.33
  262.1 3.7 copy-start.38
  262.1 3.7 copy-start.48
  275.1 157.7 %reduce-scatter.16.cloned.1.call-start = ((), (), s32[]{:S(2)}) async-start(), calls=%async_computation.11 | async-start | bytes 2359296 | tf_op jit(solution)/shard_map/reduce_scatter | solution.py:143
  281.9 156.6 %reduce-scatter.26.cloned.1.call-start = ((), (), s32[]{:S(2)}) async-start(), calls=%async_computation.16 | async-start | bytes 2359296
  293.1 1.9 copy-start.27
  293.1 191.3 %reduce-scatter.24.cloned.1.call-start = ((), (), s32[]{:S(2)}) async-start(), calls=%async_computation.15 | async-start | bytes 163840
  302.8 2.3 copy-start.35
  302.8 2.3 copy-start.2
  305.1 1.6 copy-start.4
  305.1 1.8 copy-start.14
  306.9 2.6 copy-start.40
  306.9 2.6 copy-start.42
  311.2 174.7 %reduce-scatter.22.cloned.1.call-start = ((), (), s32[]{:S(2)}) async-start(), calls=%async_computation.14 | async-start | bytes 327680
  350.7 82.5 %copy-start.7 = (f32[1,1024,512]{1,2,0:T(8,128)S(1)}, f32[1,1024,512]{1,2,0:T(8,128)}, u32[]{:S(2)}) copy-start(f32[1,1024,512]{1,2,0:T(8,128)} %copy-done.5) | copy-start | bytes 6291460
  350.7 82.5 %copy-start.50 = (f32[512]{0:T(512)S(1)}, f32[512]{0:T(512)}, u32[]{:S(2)}) copy-start(f32[512]{0:T(512)} %param.32) | copy-start | bytes 6148
  364.6 129.5 %reduce-scatter.18.cloned.1.call-start = ((), (), s32[]{:S(2)}) async-start(), calls=%async_computation.12 | async-start | bytes 327680 | tf_op jit(solution)/shard_map/reduce_scatter | solution.py:144
  432.9 76.4 %reduce-scatter.20.cloned.1.call-start = ((), (), s32[]{:S(2)}) async-start(), calls=%async_computation.13 | async-start | bytes 655360 | tf_op jit(solution)/shard_map/reduce_scatter | solution.py:144
  438.4 41.6 %copy-start.16 = (f32[1,1024,512]{1,2,0:T(8,128)S(1)}, f32[1,1024,512]{1,2,0:T(8,128)}, u32[]{:S(2)}) copy-start(f32[1,1024,512]{1,2,0:T(8,128)} %get-tuple-element.112) | copy-start | bytes 6291460
  485.2 25.7 %copy-start.1 = (f32[512,512]{1,0:T(8,128)S(1)}, f32[512,512]{1,0:T(8,128)}, u32[]{:S(2)}) copy-start(f32[512,512]{1,0:T(8,128)} %param.25) | copy-start | bytes 3145732
  (3 other events, 2.9 us)
Sparse Core Ops, SparseCore 0:
  23.3 25.8 all-gather.4
  51.1 28.5 all-gather.6
  81.6 29.2 all-gather.8
  210.2 32.9 reduce-scatter.13
  275.3 60.3 all-reduce.2
  339.2 40.4 reduce-scatter.15
  382.9 41.2 reduce-scatter.25
  427.1 19.2 reduce-scatter.23
  448.6 18.0 reduce-scatter.21
  468.9 18.1 reduce-scatter.17
  489.4 19.8 reduce-scatter.19
where the time goes:
time: 528 us; the launch traced here: 518 us
  blocking collectives  173 us (33%)
  matrix products  150 us (28%)
  local copies, waits for them, and re-layouts  77.5 us (15%)
  other arithmetic  61.4 us (12%)
  waiting for transfers between devices  38.4 us (7%)
  between operations  16.4 us (3%)
    all_gather x1, blocking collectives, shards(): lines = lax.all_gather(lines, ('dp', 'tensor'), axis=0, tiled=True)  67.5 us
    unnamed x134, local copies, waits for them, and re-layouts  59.4 us
    all_gather x4, blocking collectives, whole(): lax.all_gather(w.astype(jnp.bfloat16), 'tensor', axis=dim + 1, tiled=True)  56.8 us
    psum x1, blocking collectives, shards(): small = lax.psum(small, ('dp', 'tensor'))  37.5 us
    convert_element_type x1, other arithmetic, attend_backward(): grad_scores = (attn_probs * (grad_probs - row_delta)).astype(jnp.bfloat16)  28.7 us
    unnamed x15, waiting for transfers between devices  24.6 us
    dot_general x1, matrix products, attend_backward(): jnp.einsum('qhe,khe->hqk', grad_heads, value_heads, preferred_element_typ...  22 us
    dot_general x1, matrix products, attend_backward(): jnp.einsum('hqk,qhe->khe', probs_low, grad_heads, preferred_element_type=...  14.4 us
  transfers between devices with their start and end apart: 11, of which 2 were waited for; matrix products, arithmetic and copies ran while one was open for 42% of the time, Pallas kernels for 0%

commit v1 on v0

--- a/solution.py
+++ b/solution.py
@@ -214,7 +214,7 @@
     small = jnp.concatenate(
         [grad_gain_one, grad_bias_one, grad_gain_two, grad_bias_two, grad_b_down, grad_bias_up]
     )
-    small = lax.psum(small, ("dp", "tensor"))
+    small = lax.psum(lax.psum(small, "dp"), "tensor")
     cuts = jnp.split(small, [tokens.shape[2] * k for k in range(1, 6)])
     return (
         layer_out,

time: 528 us -> 528 us (level)
    psum x1 -> x2, blocking collectives: 37.5 us -> 38.5 us  [shards(): small = lax.psum(lax.psum(small, 'dp'), 'tensor')]
where the time goes in v1:
time: 528 us; the launch traced here: 517 us
  blocking collectives  174 us (33%)
  matrix products  150 us (28%)
  local copies, waits for them, and re-layouts  77.5 us (15%)
  other arithmetic  61.4 us (12%)
  waiting for transfers between devices  36.8 us (7%)
  between operations  16.4 us (3%)
    all_gather x1, blocking collectives, shards(): lines = lax.all_gather(lines, ('dp', 'tensor'), axis=0, tiled=True)  67.5 us
    unnamed x134, local copies, waits for them, and re-layouts  59.4 us
    all_gather x4, blocking collectives, whole(): lax.all_gather(w.astype(jnp.bfloat16), 'tensor', axis=dim + 1, tiled=True)  56.8 us
    psum x2, blocking collectives, shards(): small = lax.psum(lax.psum(small, 'dp'), 'tensor')  38.5 us
    convert_element_type x1, other arithmetic, attend_backward(): grad_scores = (attn_probs * (grad_probs - row_delta)).astype(jnp.bfloat16)  28.7 us
    unnamed x15, waiting for transfers between devices  24.6 us
    dot_general x1, matrix products, attend_backward(): jnp.einsum('qhe,khe->hqk', grad_heads, value_heads, preferred_element_typ...  22 us
    dot_general x1, matrix products, attend_backward(): jnp.einsum('hqk,qhe->khe', probs_low, grad_heads, preferred_element_type=...  14.4 us
  transfers between devices with their start and end apart: 11, of which 2 were waited for; matrix products, arithmetic and copies ran while one was open for 42% of the time, Pallas kernels for 0%

profile of v1, /device:TPU:0, one launch (start us, length us, event | category | flops | bytes accessed | tf_op | source)
XLA Modules:
  0.0 517.3 jit_solution(12495899421546429461)
XLA Ops:
  7.3 1.0 convert_element_type.127
  8.3 14.8 %all_gather.27 = bf16[3,64,512]{2,1,0:T(8,128)(2,1)} all-gather(bf16[3,64,128]{2,1,0:T(8,128)(2,1)S(1)} %convert_element_type.127), channel_id=1, replica_groups=mesh['dp'=8,'tensor'=4] {'tensor'}, dimensions={2}, use_global_device_ids=true | all-gather | bytes 245760 | tf_op jit(solution)/shard_map/all_gather | solution.py:139
  23.2 0.9 convert_element_type.138
  24.1 15.1 %all_gather.31 = bf16[64,2048]{1,0:T(8,128)(2,1)} all-gather(bf16[64,512]{1,0:T(8,128)(2,1)S(1)} %convert_element_type.138), channel_id=1, replica_groups=mesh['dp'=8,'tensor'=4] {'tensor'}, dimensions={1}, use_global_device_ids=true | all-gather | bytes 327680 | tf_op jit(solution)/shard_map/all_gather | solution.py:139
  39.3 0.9 convert_element_type.140
  40.2 14.9 %all_gather.33 = bf16[64,2048]{1,0:T(8,128)(2,1)} all-gather(bf16[64,512]{1,0:T(8,128)(2,1)S(1)} %convert_element_type.140), channel_id=1, replica_groups=mesh['dp'=8,'tensor'=4] {'tensor'}, dimensions={1}, use_global_device_ids=true | all-gather | bytes 327680 | tf_op jit(solution)/shard_map/all_gather | solution.py:139
  57.2 0.7 constant_dynamic-slice_fusion.1
  58.0 12.0 %all_gather.29 = bf16[64,512]{1,0:T(8,128)(2,1)S(1)} all-gather(bf16[64,128]{1,0:T(8,128)(2,1)S(1)} %convert_element_type.136), channel_id=1, replica_groups=mesh['dp'=8,'tensor'=4] {'tensor'}, dimensions={1}, use_global_device_ids=true | all-gather | bytes 81920 | tf_op jit(solution)/shard_map/all_gather | solution.py:139
  69.9 11.6 %all_gather.30 = bf16[512,512]{1,0:T(8,128)(2,1)} all-gather(bf16[64,512]{1,0:T(8,128)(2,1)S(1)} %all_gather.29), channel_id=1, replica_groups=mesh['dp'=8,'tensor'=4] {'dp'}, dimensions={0}, use_global_device_ids=true | all-gather | bytes 589824 | tf_op jit(solution)/shard_map/all_gather | solution.py:140
  84.5 2.3 fusion.14
  86.8 3.5 convert_bitcast_fusion
  90.7 1.0 copy-done.15
  91.7 14.0 %fusion.59 = (f32[8,1024]{1,0:T(8,128)S(1)}, f32[8,1024,1024]{1,2,0:T(8,128)}) fusion(bf16[1024,8,64]{0,2,1:T(8,128)(2,1)S(1)} %bitcast.135, bf16[1024,8,64]{0,2,1:T(8,128)(2,1)S(1)} %bitcast.133, pred[1024,1024]{0,1:T(8,128)(4,1)S(1)} %copy-done.15), kind=kOutput, calls=%fused_computation.112 | convolution fusion | flops 1098899456 | bytes 36732928 | tf_op jit(solution)/shard_map/while/body/eval_jaxpr/qhe,khe->hqk/dot_general | solution.py:64
  105.6 13.1 %fusion = f32[8,1024]{1,0:T(8,128)S(1)} fusion(f32[8,1024,1024]{1,2,0:T(8,128)} %get-tuple-element.125, f32[8,1024]{1,0:T(8,128)S(1)} %get-tuple-element.124), kind=kLoop, calls=%fused_computation.6 | loop fusion | flops 16769024 | bytes 33619968 | tf_op jit(solution)/shard_map/while/body/eval_jaxpr/reduce_sum | solution.py:77
  118.8 14.0 %fusion.29 = bf16[8,64,1024]{2,1,0:T(8,128)(2,1)S(1)} fusion(bf16[1024,8,64]{0,2,1:T(8,128)(2,1)S(1)} %bitcast.140, f32[8,1024,1024]{1,2,0:T(8,128)} %get-tuple-element.125, f32[8,1024]{1,0:T(8,128)S(1)} %fusion, f32[8,1024]{1,0:T(8,128)S(1)} %get-tuple-element.124), kind=kOutput, calls=%fused_computation.62 | convolution fusion | flops 1099431936 | bytes 35717120 | tf_op jit(solution)/shard_map/while/body/eval_jaxpr/hqk,khe->qhe/dot_general | solution.py:79
  132.9 0.8 fusion.60
  133.9 1.3 copy-done.5
  135.6 11.5 %multiply_convert_fusion.1 = (bf16[1024,2048]{1,0:T(8,128)(2,1)}, f32[1024,2048]{1,0:T(8,128)}) fusion(f32[2048]{0:T(1024)S(1)} %copy-done.46, bf16[512,2048]{1,0:T(8,128)(2,1)} %all-gather.7.cloned.1.call-done, f32[1,1024,512]{1,2,0:T(8,128)} %copy-done.5, f32[512]{0:T(512)S(1)} %copy-done.49, f32[512]{0:T(512)S(1)} %copy-done.43, f32[1024]{0:T(1024)S(1)} %fusion.40, ...), kind=kOutput, calls=%fused_computation.21 | convolution fusion | flops 2171076608 | bytes 16797696 | tf_op jit(solution)/shard_map/nsd,df->nsf/dot_general | solution.py:172
  147.1 10.2 %convert_reduce_fusion = (f32[2048]{0:T(1024)S(1)}, bf16[1024,2048]{1,0:T(8,128)(2,1)S(1)}) fusion(f32[1024,2048]{1,0:T(8,128)} %get-tuple-element.129, f32[2048]{0:T(1024)S(1)} %copy-done.46, bf16[512,2048]{1,0:T(8,128)(2,1)} %all-gather.9.cloned.1.call-done, bf16[1,1024,512]{2,1,0:T(8,128)(2,1)S(1)} %copy-done.24), kind=kOutput, calls=%fused_computation.20 | convolution fusion | flops 2195716096 | bytes 15745024 | tf_op jit(solution)/shard_map/nsd,df->nsf/dot_general | solution.py:179
  157.3 3.7 fusion.62
  161.0 2.9 copy.79
  163.9 3.0 fusion.16
  168.4 0.9 copy-done.3
  169.3 0.7 copy-done.53
  170.0 1.6 convolution_convert_fusion.4
  171.6 2.0 convolution_convert_fusion.3
  173.6 14.4 %fusion.25 = bf16[8,64,1024]{2,1,0:T(8,128)(2,1)} fusion(bf16[1024,8,64]{0,2,1:T(8,128)(2,1)S(1)} %bitcast.138, f32[8,1024,1024]{1,2,0:T(8,128)} %get-tuple-element.125, f32[8,1024]{1,0:T(8,128)S(1)} %log_add_fusion), kind=kOutput, calls=%fused_computation.59 | convolution fusion | flops 1091043328 | bytes 35684352 | tf_op jit(solution)/shard_map/while/body/eval_jaxpr/hqk,qhe->khe/dot_general | solution.py:91
  188.0 22.0 %multiply_reduce_fusion = (f32[8,1024]{1,0:T(8,128)S(1)}, f32[8,1024,1024]{1,2,0:T(8,128)}) fusion(f32[8,1024,1024]{1,2,0:T(8,128)} %get-tuple-element.125, f32[8,1024]{1,0:T(8,128)S(1)} %log_add_fusion, bf16[1024,8,64]{0,2,1:T(8,128)(2,1)S(1)} %bitcast.139, bf16[1024,8,64]{0,2,1:T(8,128)(2,1)S(1)} %bitcast.141), kind=kOutput, calls=%fused_computation.1 | convolution fusion | flops 1098899456 | bytes 69271552 | tf_op jit(solution)/shard_map/while/body/eval_jaxpr/qhe,khe->hqk/dot_general | solution.py:94
  210.0 28.7 %multiply_convert_fusion = bf16[8,1024,1024]{1,2,0:T(8,128)(2,1)} fusion(f32[8,1024,1024]{1,2,0:T(8,128)} %get-tuple-element.131, f32[8,1024,1024]{1,2,0:T(8,128)} %get-tuple-element.125, f32[8,1024]{1,0:T(8,128)S(1)} %get-tuple-element.130, f32[8,1024]{1,0:T(8,128)S(1)} %log_add_fusion), kind=kLoop, calls=%fused_computation | loop fusion | flops 33554432 | bytes 83951616 | tf_op jit(solution)/shard_map/while/body/eval_jaxpr/convert_element_type | solution.py:98
  238.8 12.1 %multiply_convert_fusion.2 = bf16[8,64,1024]{2,1,0:T(8,128)(2,1)} fusion(bf16[1024,8,64]{0,2,1:T(8,128)(2,1)S(1)} %bitcast.136, bf16[8,1024,1024]{1,2,0:T(8,128)(2,1)} %multiply_convert_fusion), kind=kOutput, calls=%fused_computation.47 | convolution fusion | flops 1074790400 | bytes 18874368 | tf_op jit(solution)/shard_map/while/body/eval_jaxpr/hqk,qhe->khe/dot_general | solution.py:105
  250.8 9.9 %multiply_convert_fusion.3 = bf16[8,64,1024]{2,1,0:T(8,128)(2,1)} fusion(bf16[1024,8,64]{0,2,1:T(8,128)(2,1)S(1)} %bitcast.134, bf16[8,1024,1024]{1,2,0:T(8,128)(2,1)} %multiply_convert_fusion), kind=kOutput, calls=%fused_computation.48 | convolution fusion | flops 1074790400 | bytes 18874368 | tf_op jit(solution)/shard_map/while/body/eval_jaxpr/hqk,khe->qhe/dot_general | solution.py:101
  260.7 1.3 copy.85
  262.0 2.4 copy.83
  264.4 1.3 copy.84
  265.8 4.8 fusion.28
  270.6 4.4 copy.89
  275.1 6.6 %convolution_convert_fusion.1 = bf16[512,2048]{1,0:T(8,128)(2,1)} fusion(bf16[1024,2048]{1,0:T(8,128)(2,1)} %copy-done.55, f32[1,1024,512]{1,2,0:T(8,128)} %copy-done.5, f32[512]{0:T(512)S(1)} %copy-done.49, f32[512]{0:T(512)S(1)} %copy-done.43, f32[1024]{0:T(1024)S(1)} %fusion.40, f32[1024]{0:T(1024)S(1)} %broadcast_multiply_fusion), kind=kOutput, calls=%fused_computation.30 | convolution fusion | flops 2151153664 | bytes 8400896 | tf_op jit(solution)/shard_map/nsd,nsf->df/dot_general | solution.py:183
  282.0 0.9 copy-done.25
  283.0 6.0 %fusion.15 = bf16[512,2048]{0,1:T(8,128)(2,1)} fusion(bf16[1024,2048]{1,0:T(8,128)(2,1)} %get-tuple-element.128, bf16[1,1024,512]{2,1,0:T(8,128)(2,1)S(1)} %copy-done.25), kind=kOutput, calls=%fused_computation.31 | convolution fusion | flops 2148532224 | bytes 7340032 | tf_op jit(solution)/shard_map/nsd,nsf->df/dot_general | solution.py:178
  289.0 4.0 copy.110
  294.9 4.9 fusion.61
  299.8 2.9 copy.86
  302.7 2.3 fusion.18
  305.0 1.0 fusion.17
  306.8 2.6 fusion.55
  309.5 1.6 copy.108
  311.2 24.4 %all-reduce.3.cloned.1.call-done = bf16[3,512,512]{2,0,1:T(4,128)(2,1)} async-done(((bf16[3,512,512]{2,0,1:T(4,128)(2,1)}), bf16[3,512,512]{2,0,1:T(4,128)(2,1)}) %all-reduce.3.cloned.1.call-update) | async-done | bytes 1572880
  335.6 1.0 constant_dynamic-slice_fusion
  336.6 14.0 %copy.106 = bf16[3,64,512]{0,1,2:T(8,128)(2,1)} copy(bf16[3,64,512]{2,0,1:T(4,128)(2,1)S(1)} %constant_dynamic-slice_fusion) | data formatting | bytes 393216
  350.6 13.9 %reshape.435 = bf16[512,192]{1,0:T(8,128)(2,1)} reshape(bf16[512,64,3]{2,1,0:T(8,128)(2,1)} %bitcast.132) | data formatting | bytes 393216
  364.6 67.5 %all-gather = f32[32,1,1024]{2,1,0:T(1,128)S(1)} all-gather(f32[1,1,1024]{2,1,0:T(1,128)S(1)} %maximum_bitcast_fusion), channel_id=1, replica_groups=mesh['dp'=8,'tensor'=4] {'dp','tensor'}, dimensions={0}, use_global_device_ids=true | all-gather | bytes 135168 | tf_op jit(solution)/shard_map/all_gather | solution.py:210
  433.1 5.2 %fusion.21 = bf16[1,1024,512]{1,2,0:T(8,128)(2,1)S(1)} fusion(f32[1,1024,512]{1,2,0:T(8,128)S(1)} %copy-done.7, bf16[1024,2048]{1,0:T(8,128)(2,1)} %get-tuple-element.128, bf16[512,2048]{1,0:T(8,128)(2,1)} %all-gather.9.cloned.1.call-done, f32[512]{0:T(512)S(1)} %copy-done.50), kind=kOutput, calls=%fused_computation.44 | convolution fusion | flops 2149056512 | bytes 9439232 | tf_op jit(solution)/shard_map/nsf,df->nsd/dot_general | solution.py:175
  438.4 2.1 copy.111
  440.5 1.3 copy.92
  441.8 22.7 %psum.14 = f32[4608]{0:T(1024)S(1)} all-reduce(f32[4608]{0:T(1024)S(1)} %constant_dynamic-update-slice_fusion), channel_id=1, replica_groups=mesh['dp'=8,'tensor'=4] {'dp'}, use_global_device_ids=true, to_apply=%region_27.28 | all-reduce | flops 4608 | bytes 36864 | tf_op jit(solution)/shard_map/psum | solution.py:217
  464.6 15.8 %psum.15 = f32[4608]{0:T(1024)S(1)} all-reduce(f32[4608]{0:T(1024)S(1)} %psum.14), channel_id=1, replica_groups=mesh['dp'=8,'tensor'=4] {'tensor'}, use_global_device_ids=true, to_apply=%region_28.29 | all-reduce | flops 4608 | bytes 36864 | tf_op jit(solution)/shard_map/psum | solution.py:217
  480.9 1.8 copy.93
  483.3 2.0 fusion.36
  485.4 0.8 copy.109
  486.8 5.3 %reshape.436 = bf16[128,64,3]{2,1,0:T(8,128)(2,1)S(1)} reshape(bf16[128,192]{1,0:T(8,128)(2,1)} %reduce-scatter.22.cloned.1.call-done) | data formatting | bytes 98304
  492.1 2.2 copy.107
  495.0 1.5 convert_element_type.154
  496.5 12.2 %reduce-scatter.20.cloned.1.call-done = bf16[64,512]{0,1:T(8,128)(2,1)} async-done(((bf16[64,2048]{0,1:T(8,128)(2,1)}), bf16[64,512]{0,1:T(8,128)(2,1)}) %reduce-scatter.20.cloned.1.call-update) | async-done | bytes 65552 | tf_op jit(solution)/shard_map/reduce_scatter | solution.py:144
  508.7 1.6 copy.95
  (176 shorter events, 12.8 us)
Async XLA Ops:
  7.2 74.9 %copy-start = (f32[512,512]{1,0:T(8,128)S(1)}, f32[512,512]{1,0:T(8,128)}, u32[]{:S(2)}) copy-start(f32[512,512]{1,0:T(8,128)} %param.25) | copy-start | bytes 3145732
  7.2 48.7 %copy-start.51 = (s32[4]{0:T(128)S(1)}, s32[4]{0:T(128)}, u32[]{:S(2)}) copy-start(s32[4]{0:T(128)} %param.20) | copy-start | bytes 52
  7.2 50.7 %copy-start.36 = (f32[64,128]{1,0:T(8,128)S(1)}, f32[64,128]{1,0:T(8,128)}, u32[]{:S(2)}) copy-start(f32[64,128]{1,0:T(8,128)} %param.22) | copy-start | bytes 98308
  7.2 74.4 %copy-start.22 = (bf16[1,1024,512]{2,1,0:T(8,128)(2,1)S(1)}, bf16[1,1024,512]{2,1,0:T(8,128)(2,1)}, u32[]{:S(2)}) copy-start(bf16[1,1024,512]{2,1,0:T(8,128)(2,1)} %param.17) | copy-start | bytes 3145732
  7.2 79.6 %all-gather.5.cloned.1.call-start = ((), (), s32[]{:S(2)}) async-start(), calls=%async_computation.7 | async-start | bytes 1769472 | tf_op jit(solution)/shard_map/all_gather | solution.py:140
  23.1 112.4 %all-gather.7.cloned.1.call-start = ((), (), s32[]{:S(2)}) async-start(), calls=%async_computation.8 | async-start | bytes 2359296 | tf_op jit(solution)/shard_map/all_gather | solution.py:140
  39.2 107.8 %all-gather.9.cloned.1.call-start = ((), (), s32[]{:S(2)}) async-start(), calls=%async_computation.9 | async-start | bytes 2359296 | tf_op jit(solution)/shard_map/all_gather | solution.py:140
  55.1 27.6 %copy-start.44 = (f32[512]{0:T(512)S(1)}, f32[512]{0:T(512)}, u32[]{:S(2)}) copy-start(f32[512]{0:T(512)} %param.26) | copy-start | bytes 6148
  55.2 254.3 %reduce-scatter.14.cloned.1.call-start = ((), (), s32[]{:S(2)}) async-start(), calls=%async_computation.10 | async-start | bytes 589824 | tf_op jit(solution)/shard_map/reduce_scatter | solution.py:143
  57.2 25.6 %copy-start.41 = (f32[1,256]{1,0:T(1,128)}, f32[1,256]{1,0:T(1,128)S(1)}, u32[]{:S(2)}) copy-start(f32[1,256]{1,0:T(1,128)S(1)} %get-tuple-element.139) | copy-start | bytes 3076
  57.2 25.6 %copy-start.39 = (f32[1,256]{1,0:T(1,128)}, f32[1,256]{1,0:T(1,128)S(1)}, u32[]{:S(2)}) copy-start(f32[1,256]{1,0:T(1,128)S(1)} %get-tuple-element.138) | copy-start | bytes 3076
  82.7 1.2 copy-start.23
  83.1 3.7 copy-start.30
  83.1 3.7 copy-start.37
  83.1 3.7 copy-start.47
  83.5 6.8 %copy-start.34 = (f32[1024]{0:T(1024)}, f32[1024]{0:T(1024)S(1)}, u32[]{:S(2)}) copy-start(f32[1024]{0:T(1024)S(1)} %multiply_reduce_fusion.2) | copy-start | bytes 12292
  84.0 6.3 %copy-start.32 = (f32[1024]{0:T(1024)}, f32[1024]{0:T(1024)S(1)}, u32[]{:S(2)}) copy-start(f32[1024]{0:T(1024)S(1)} %fusion.39) | copy-start | bytes 12292
  84.5 83.5 %copy-start.13 = (bf16[1,1024,512]{1,2,0:T(8,128)(2,1)}, bf16[1,1024,512]{1,2,0:T(8,128)(2,1)S(1)}, u32[]{:S(2)}) copy-start(bf16[1,1024,512]{1,2,0:T(8,128)(2,1)S(1)} %copy.78) | copy-start | bytes 3145732
  90.3 1.4 copy-start.15
  90.6 15.0 %copy-start.9 = (bf16[1,1,1024,512]{2,3,0,1:T(8,128)(2,1)}, bf16[1,1,1024,512]{2,3,0,1:T(8,128)(2,1)S(1)}, u32[]{:S(2)}) copy-start(bf16[1,1,1024,512]{2,3,0,1:T(8,128)(2,1)S(1)} %get-tuple-element.115) | copy-start | bytes 3145732
  90.7 15.0 %copy-start.11 = (bf16[1,1,1024,512]{2,3,0,1:T(8,128)(2,1)}, bf16[1,1,1024,512]{2,3,0,1:T(8,128)(2,1)S(1)}, u32[]{:S(2)}) copy-start(bf16[1,1,1024,512]{2,3,0,1:T(8,128)(2,1)S(1)} %get-tuple-element.116) | copy-start | bytes 3145732
  90.7 28.1 %copy-start.17 = (bf16[1,1,1024,512]{2,3,0,1:T(8,128)(2,1)}, bf16[1,1,1024,512]{2,3,0,1:T(8,128)(2,1)S(1)}, u32[]{:S(2)}) copy-start(bf16[1,1,1024,512]{2,3,0,1:T(8,128)(2,1)S(1)} %get-tuple-element.117) | copy-start | bytes 3145732
  118.8 14.1 %copy-start.28 = (bf16[512,512]{1,0:T(8,128)(2,1)S(1)}, bf16[512,512]{1,0:T(8,128)(2,1)}, u32[]{:S(2)}) copy-start(bf16[512,512]{1,0:T(8,128)(2,1)} %all_gather.30) | copy-start | bytes 1572868
  133.8 1.3 copy-start.5
  133.8 1.7 copy-start.43
  133.8 1.7 copy-start.46
  133.8 1.7 copy-start.49
  135.5 11.6 %copy-start.24 = (bf16[1,1024,512]{2,1,0:T(8,128)(2,1)S(1)}, bf16[1,1024,512]{2,1,0:T(8,128)(2,1)}, u32[]{:S(2)}) copy-start(bf16[1,1024,512]{2,1,0:T(8,128)(2,1)} %param.33) | copy-start | bytes 3145732
  147.1 10.3 %copy-start.45 = (bf16[512,2048]{1,0:T(8,128)(2,1)S(1)}, bf16[512,2048]{1,0:T(8,128)(2,1)}, u32[]{:S(2)}) copy-start(bf16[512,2048]{1,0:T(8,128)(2,1)} %all-gather.7.cloned.1.call-done) | copy-start | bytes 6291460
  157.3 3.7 copy-start.55
  163.9 3.0 copy-start.6
  163.9 3.5 copy-start.8
  168.0 1.3 copy-start.3
  168.0 2.0 copy-start.53
  170.0 1.6 copy-start.21
  170.0 1.6 copy-start.29
  173.6 14.4 %copy-start.18 = (bf16[1,1,1024,512]{2,3,0,1:T(8,128)(2,1)S(1)}, bf16[1,1,1024,512]{2,3,0,1:T(8,128)(2,1)}, u32[]{:S(2)}) copy-start(bf16[1,1,1024,512]{2,3,0,1:T(8,128)(2,1)} %copy-done.17) | copy-start | bytes 3145732
  210.0 125.6 %all-reduce.3.cloned.1.call-start = ((), (), s32[]{:S(2)}) async-start(), calls=%async_computation.17 | async-start | bytes 4194304
  210.0 28.7 %copy-start.12 = (bf16[1,1,1024,512]{2,3,0,1:T(8,128)(2,1)S(1)}, bf16[1,1,1024,512]{2,3,0,1:T(8,128)(2,1)}, u32[]{:S(2)}) copy-start(bf16[1,1,1024,512]{2,3,0,1:T(8,128)(2,1)} %copy-done.11) | copy-start | bytes 3145732
  238.8 12.1 %copy-start.10 = (bf16[1,1,1024,512]{2,3,0,1:T(8,128)(2,1)S(1)}, bf16[1,1,1024,512]{2,3,0,1:T(8,128)(2,1)}, u32[]{:S(2)}) copy-start(bf16[1,1,1024,512]{2,3,0,1:T(8,128)(2,1)} %copy-done.9) | copy-start | bytes 3145732
  250.8 9.9 %copy-start.19 = (bf16[8,64,1024]{2,1,0:T(8,128)(2,1)S(1)}, bf16[8,64,1024]{2,1,0:T(8,128)(2,1)}, u32[]{:S(2)}) copy-start(bf16[8,64,1024]{2,1,0:T(8,128)(2,1)} %fusion.25) | copy-start | bytes 3145732
  260.7 3.7 copy-start.20
  262.0 3.7 copy-start.26
  262.0 3.7 copy-start.31
  262.0 3.7 copy-start.33
  262.0 3.7 copy-start.38
  262.0 3.7 copy-start.48
  275.0 157.7 %reduce-scatter.16.cloned.1.call-start = ((), (), s32[]{:S(2)}) async-start(), calls=%async_computation.11 | async-start | bytes 2359296 | tf_op jit(solution)/shard_map/reduce_scatter | solution.py:143
  281.8 156.6 %reduce-scatter.26.cloned.1.call-start = ((), (), s32[]{:S(2)}) async-start(), calls=%async_computation.16 | async-start | bytes 2359296
  293.0 1.9 copy-start.27
  293.0 192.4 %reduce-scatter.24.cloned.1.call-start = ((), (), s32[]{:S(2)}) async-start(), calls=%async_computation.15 | async-start | bytes 163840
  302.7 2.3 copy-start.35
  302.7 2.3 copy-start.2
  305.0 1.6 copy-start.4
  305.0 1.8 copy-start.14
  306.8 2.6 copy-start.40
  306.8 2.6 copy-start.42
  311.1 175.7 %reduce-scatter.22.cloned.1.call-start = ((), (), s32[]{:S(2)}) async-start(), calls=%async_computation.14 | async-start | bytes 327680
  350.6 82.5 %copy-start.7 = (f32[1,1024,512]{1,2,0:T(8,128)S(1)}, f32[1,1024,512]{1,2,0:T(8,128)}, u32[]{:S(2)}) copy-start(f32[1,1024,512]{1,2,0:T(8,128)} %copy-done.5) | copy-start | bytes 6291460
  350.6 82.5 %copy-start.50 = (f32[512]{0:T(512)S(1)}, f32[512]{0:T(512)}, u32[]{:S(2)}) copy-start(f32[512]{0:T(512)} %param.32) | copy-start | bytes 6148
  364.5 130.5 %reduce-scatter.18.cloned.1.call-start = ((), (), s32[]{:S(2)}) async-start(), calls=%async_computation.12 | async-start | bytes 327680 | tf_op jit(solution)/shard_map/reduce_scatter | solution.py:144
  432.8 75.9 %reduce-scatter.20.cloned.1.call-start = ((), (), s32[]{:S(2)}) async-start(), calls=%async_computation.13 | async-start | bytes 655360 | tf_op jit(solution)/shard_map/reduce_scatter | solution.py:144
  438.3 42.6 %copy-start.16 = (f32[1,1024,512]{1,2,0:T(8,128)S(1)}, f32[1,1024,512]{1,2,0:T(8,128)}, u32[]{:S(2)}) copy-start(f32[1,1024,512]{1,2,0:T(8,128)} %get-tuple-element.112) | copy-start | bytes 6291460
  486.2 24.1 %copy-start.1 = (f32[512,512]{1,0:T(8,128)S(1)}, f32[512,512]{1,0:T(8,128)}, u32[]{:S(2)}) copy-start(f32[512,512]{1,0:T(8,128)} %param.25) | copy-start | bytes 3145732
  (3 other events, 2.9 us)
Sparse Core Ops, SparseCore 0:
  23.3 25.8 all-gather.4
  51.1 28.5 all-gather.6
  81.6 29.2 all-gather.8
  210.1 32.9 reduce-scatter.13
  275.2 60.3 all-reduce.2
  339.1 40.4 reduce-scatter.15
  382.8 41.2 reduce-scatter.25
  427.0 19.2 reduce-scatter.23
  448.5 17.8 reduce-scatter.21
  468.6 17.8 reduce-scatter.17
  488.8 19.7 reduce-scatter.19
